TPU v7x, 256 devices: a whole 4x4x8 slice. The times are simulated.
256 devices in a mesh: context: 32 (over y, z), head: 2 (over core), dp: 4 (over x).
Axes of the slice: x: 4, y: 4, z: 8, core: 2. Of those that a mesh axis runs over, the one named last changes fastest.
Arguments:
- lin_query: float32 [16384, 4096], P(('dp', 'context'), 'head'), parts along dimension 0, may hold values from -6 to 6
- lin_key: float32 [16384, 4096], P(('dp', 'context'), 'head'), parts along dimension 0, may hold values from -6 to 6
- lin_value: float32 [16384, 4096], P(('dp', 'context'), 'head'), parts along dimension 0, may hold values from -6 to 6
- lin_gate: float32 [16384, 4096], P(('dp', 'context'), 'head'), parts along dimension 0, may hold values from -8 to 8
- decay_rate: float32 [32, 16384], P('head', ('dp', 'context')), parts along dimension 1, may hold values from 0 to 1.5, as said below
- norm_gain: float32 [4096], P('head'), may hold values from 0.5 to 1.5
- sm_query: float32 [16384, 4096], P(('dp', 'context'), 'head'), parts along dimension 0, may hold values from -24 to 24
- sm_key: float32 [16384, 512], P(('dp', 'context'), 'head'), parts along dimension 0, may hold values from -24 to 24
- sm_value: float32 [16384, 512], P(('dp', 'context'), 'head'), parts along dimension 0, may hold values from -6 to 6
- doc_lengths: int32 [64], P('dp'), parts along dimension 0, may hold values from 1 to 3072, 4096 in all
Outputs:
- lin_out: float32 [16384, 4096], P(('dp', 'context'), 'head'), parts along dimension 0
- sm_out: float32 [16384, 4096], P(('dp', 'context'), 'head'), parts along dimension 0
There are 4 independent parts, one for each index of `dp`. A program takes and returns all parts, laid end to end along the dimension named above; an argument that names none is the same for every part. Nothing has to cross between parts.
Inputs may be any that keep to these rules, and one draw needn't show every extreme that they name: `doc_lengths`: the 16 lengths sum to 4096 and the longest is exactly 3072. `decay_rate`: positive rates.
All inputs are finite; a program needn't handle non-finite values.
Results may differ from a plain program's by a relative error of at most 0.0003.
Values sent between devices are 32-bit elements; how exact they have to be, the bound alone decides.
No kernel may reach another device: no remote copies, remote signals or barrier semaphores. Data moves between devices by JAX's collectives and lax.ppermute only.
A program may use at most 192 MiB of HBM per device.

v0:
```python
import jax
import jax.numpy as jnp
from jax import lax
from jax.sharding import PartitionSpec as P

HEAD_DIM = 128
ROT_DIM = 64
rope_base = 10000000.0
norm_eps = 1e-05
highest = lax.Precision.HIGHEST


def entering(value, axis, join, neutral):
    count, mine = (lax.axis_size(axis), lax.axis_index(axis))
    pieces = jax.tree.map(lambda part: lax.all_gather(part, axis), value)
    subtotal = jax.tree.map(
        lambda part, zero: jnp.full_like(part, 0) + jnp.asarray(zero, part.dtype), value, neutral
    )

    def turn(position, subtotal):
        longer = join(subtotal, jax.tree.map(lambda part: part[position], pieces))
        return jax.tree.map(lambda new, old: jnp.where(position < mine, new, old), longer, subtotal)

    return lax.fori_loop(0, count - 1, turn, subtotal)


def doc_tables(doc_lengths):
    doc_ends = jnp.cumsum(doc_lengths)
    doc_starts = doc_ends - doc_lengths
    return (doc_starts, doc_ends)


def doc_number(tokens_at, doc_ends):
    return jnp.sum((doc_ends[None, :] <= tokens_at[:, None]).astype(jnp.int32), axis=1)


def doc_begin(tokens_at, doc_starts):
    picked = jnp.where(doc_starts[None, :] <= tokens_at[:, None], doc_starts[None, :], 0)
    return jnp.max(picked, axis=1)


def lightning_block(
    query_heads, key_heads, value_heads, forgetting_factors, first_token, doc_starts, doc_ends
):
    width = query_heads.shape[1]
    tokens_at = first_token + jnp.arange(width, dtype=jnp.int32)
    doc_ids = doc_number(tokens_at, doc_ends)
    begins = doc_begin(tokens_at, doc_starts)
    log_decay = jnp.cumsum(-forgetting_factors, axis=1)
    visible = (doc_ids[:, None] == doc_ids[None, :]) & (tokens_at[:, None] >= tokens_at[None, :])
    spread = jnp.where(visible[None], log_decay[:, :, None] - log_decay[:, None, :], 0.0)
    weight = jnp.where(visible[None], jnp.exp(spread), 0.0)
    scores = jnp.einsum("htd,hsd->hts", query_heads, key_heads, precision=highest) * weight
    intra = jnp.einsum("hts,hsd->htd", scores, value_heads, precision=highest)
    carried_rows = begins < first_token
    block_decay = jnp.where(carried_rows[-1], jnp.exp(log_decay[:, -1]), 0.0)
    in_tail = doc_ids == doc_ids[-1]
    tail_gap = jnp.where(in_tail[None], log_decay[:, -1:] - log_decay, 0.0)
    tail_weight = jnp.where(in_tail[None], jnp.exp(tail_gap), 0.0)
    block_inner = jnp.einsum(
        "htd,hte->hde", key_heads * tail_weight[:, :, None], value_heads, precision=highest
    )
    return (intra, log_decay, carried_rows, block_decay, block_inner)


def carried_term(query_heads, state, log_decay, carried_rows):
    reach_weight = jnp.where(carried_rows[None], jnp.exp(log_decay), 0.0)
    return (
        jnp.einsum("htd,hde->hte", query_heads, state, precision=highest) * reach_weight[:, :, None]
    )


def finish(attention, lin_gate, norm_gain):
    rows_count = attention.shape[0]
    per_head = attention.reshape(rows_count, -1, HEAD_DIM)
    mean_square = jnp.mean(per_head * per_head, axis=-1, keepdims=True)
    normed = (per_head / jnp.sqrt(mean_square + norm_eps)).reshape(rows_count, -1)
    return normed * norm_gain[None, :] * jax.nn.sigmoid(lin_gate)


def rotate(heads_in, positions):
    half = ROT_DIM // 2
    inverse = rope_base ** (-(2.0 * jnp.arange(half, dtype=jnp.float32)) / ROT_DIM)
    angle = positions.astype(jnp.float32)[:, None] * inverse[None, :]
    cosine = jnp.cos(angle)[:, None, :]
    sine = jnp.sin(angle)[:, None, :]
    first_half = heads_in[..., :half]
    second_half = heads_in[..., half:ROT_DIM]
    return jnp.concatenate(
        [
            first_half * cosine - second_half * sine,
            second_half * cosine + first_half * sine,
            heads_in[..., ROT_DIM:],
        ],
        axis=-1,
    )


def combine_states(earlier, later):
    return (earlier[0] * later[0], later[0][:, None, None] * earlier[1] + later[1])


def shards(
    lin_query,
    lin_key,
    lin_value,
    lin_gate,
    decay_rate,
    norm_gain,
    sm_query,
    sm_key,
    sm_value,
    doc_lengths,
):
    rows_here = lin_query.shape[0]
    lin_heads = lin_query.shape[1] // HEAD_DIM
    kv_local = sm_key.shape[1] // HEAD_DIM
    group = lin_heads // kv_local
    first_token = lax.axis_index("context") * rows_here
    doc_starts, doc_ends = doc_tables(doc_lengths)

    def split_heads(matrix):
        return matrix.reshape(rows_here, -1, HEAD_DIM).transpose(1, 0, 2)

    query_heads = split_heads(lin_query)
    intra, log_decay, carried_rows, block_decay, block_inner = lightning_block(
        query_heads,
        split_heads(lin_key),
        split_heads(lin_value),
        decay_rate,
        first_token,
        doc_starts,
        doc_ends,
    )
    identity = (jnp.ones_like(block_decay), jnp.zeros_like(block_inner))
    prior = entering((block_decay, block_inner), "context", combine_states, identity)
    state = prior[1]
    attention = intra + carried_term(query_heads, state, log_decay, carried_rows)
    attention = attention.transpose(1, 0, 2).reshape(rows_here, lin_heads * HEAD_DIM)
    lin_out = finish(attention, lin_gate, norm_gain)
    tokens_at = first_token + jnp.arange(rows_here, dtype=jnp.int32)
    positions = tokens_at - doc_begin(tokens_at, doc_starts)
    row_docs = doc_number(tokens_at, doc_ends)
    first_begin = doc_begin(first_token[None], doc_starts)[0]
    last_token = first_token + rows_here - 1
    queries = rotate(sm_query.reshape(rows_here, lin_heads, HEAD_DIM), positions)
    queries = queries.reshape(rows_here, kv_local, group, HEAD_DIM).transpose(1, 2, 0, 3)
    keys_rot = rotate(sm_key.reshape(rows_here, kv_local, HEAD_DIM), positions).reshape(
        rows_here, kv_local * HEAD_DIM
    )
    stacked = jnp.stack([keys_rot, sm_value])
    scale = HEAD_DIM ** (-0.5)
    start_carry = (
        jnp.full((kv_local, group, rows_here), -1e30, jnp.float32),
        jnp.zeros((kv_local, group, rows_here), jnp.float32),
        jnp.zeros((kv_local, group, rows_here, HEAD_DIM), jnp.float32),
    )
    piece = lax.all_gather(stacked, "context", axis=1, tiled=True)
    start = jnp.int32(0)
    count = piece.shape[1]
    relevant = (start <= last_token) & (start + count - 1 >= first_begin)

    def attend(current):
        top_old, total_old, summed_old = current
        key_index = jnp.arange(count, dtype=jnp.int32)
        key_docs = doc_number(key_index, doc_ends)
        visible = (
            (key_index[None, :] >= 0)
            & (key_docs[None, :] == row_docs[:, None])
            & (key_index[None, :] <= tokens_at[:, None])
        )
        key_rows = piece[0].reshape(count, kv_local, HEAD_DIM)
        value_rows = piece[1].reshape(count, kv_local, HEAD_DIM)
        scores = jnp.einsum("kgqd,nkd->kgqn", queries, key_rows, precision=highest) * scale
        masked = jnp.where(visible[None, None], scores, -jnp.inf)
        top_new = jnp.maximum(top_old, jnp.max(masked, axis=-1))
        weights = jnp.where(visible[None, None], jnp.exp(masked - top_new[..., None]), 0.0)
        total_new = jnp.sum(weights, axis=-1)
        summed_new = jnp.einsum("kgqn,nkd->kgqd", weights, value_rows, precision=highest)
        return (top_new, total_new, summed_new)

    def keep(current):
        return current

    final_carry = lax.cond(relevant, attend, keep, start_carry)
    mixed = final_carry[2] / final_carry[1][..., None]
    sm_out = mixed.transpose(2, 0, 1, 3).reshape(rows_here, lin_heads * HEAD_DIM)
    return (lin_out, sm_out)


def solution(mesh):
    in_specs = (
        P(("dp", "context"), "head"),
        P(("dp", "context"), "head"),
        P(("dp", "context"), "head"),
        P(("dp", "context"), "head"),
        P("head", ("dp", "context")),
        P("head"),
        P(("dp", "context"), "head"),
        P(("dp", "context"), "head"),
        P(("dp", "context"), "head"),
        P("dp"),
    )
    out_specs = (P(("dp", "context"), "head"), P(("dp", "context"), "head"))
    return jax.shard_map(shards, mesh=mesh, in_specs=in_specs, out_specs=out_specs, check_vma=False)
```

profile of v0, /device:TPU:1, one launch (start us, length us, event | category | flops | bytes accessed | tf_op | source)
XLA Modules:
  0.0 413.0 jit_solution(14850499489194038331)
XLA Ops:
  7.2 0.8 copy.87
  8.2 1.3 fusion.22
  9.7 1.0 copy.114
  10.7 1.0 copy.95
  11.9 0.7 pad_maximum_fusion.1
  12.7 0.6 slice.38
  13.2 0.6 broadcast_compare_fusion
  13.9 0.6 slice.36
  14.5 0.7 neg.14
  15.2 1.5 copy.111
  17.0 0.9 slice_reduce_fusion
  18.0 3.4 fusion.15
  21.6 1.4 copy.121
  23.3 1.3 copy.117
  25.3 1.3 dynamic-slice
  27.5 65.1 %all-reduce = f32[512]{0:T(512)S(1)} all-reduce(f32[512]{0:T(512)S(1)} %dynamic-update-slice), channel_id=2, replica_groups=mesh['context'=32,'head'=2,'dp'=4] {'context'}, use_global_device_ids=true, to_apply=%add | all-reduce | flops 512 | bytes 4096
  92.7 1.4 copy.120
  94.4 0.6 multiply_subtract_fusion
  95.1 2.9 pad_maximum_fusion
  98.1 2.5 convolution_multiply_fusion
  100.6 2.0 convolution_bitcast_fusion.1
  102.6 15.6 %all-gather.5.cloned.1.call-done = f32[2,4096,256]{1,2,0:T(8,128)} async-done(((f32[2,128,256]{1,2,0:T(8,128)}), f32[2,4096,256]{1,2,0:T(8,128)}) %all-gather.5.cloned.1.call-update) | async-done | bytes 8388624 | tf_op jit(solution)/shard_map/all_gather | solution.py:158
  118.3 91.8 %conditional.1 = (f32[2,8,128]{2,1,0:T(8,128)S(1)}, f32[2,8,128,128]{3,2,1,0:T(8,128)S(1)}) conditional(s32[]{:T(128)} %convert_element_type.19, () %tuple.31, (s32[16]{0:T(128)S(1)}, s32[128]{0:T(128)S(1)}, s32[]{:T(128)}, s32[128]{0:T(128)S(1)}, f32[2,4096,256]{1,2,0:T(8,128)}, /*index=5*/f32[2,8,128,128]{3,2,1,0:T(8,128)}) %tuple.67), branch_computations={%region_8.9_spmd, %region_9.13_spmd} | conditional | flops 25872230400 | bytes 130107472 | solution.py:185
  118.9 4.0 fusion.23
  122.9 35.2 %fusion = (f32[2,8,128]{2,1,0:T(8,128)S(1)}, f32[2,8,128,4096]{3,2,1,0:T(8,128)}) fusion(pred[128,4096]{1,0:T(8,128)(4,1)S(1)} %fusion.8, f32[2,8,128,128]{3,2,1,0:T(8,128)} %get-tuple-element.111, f32[4096,2,128,1]{0,2,3,1:T(8,128)S(1)} %bitcast.95), kind=kOutput, calls=%fused_computation.2 | convolution fusion | flops 12910065664 | bytes 39329792 | tf_op jit(solution)/shard_map/cond/branch_1_fun/kgqd,nkd->kgqn/dot_general | solution.py:174
  158.1 35.1 %fusion.1 = f32[2,8,128,128]{3,2,1,0:T(8,128)S(1)} fusion(f32[4096,2,128,1]{0,2,3,1:T(8,128)S(1)} %bitcast.103, f32[2,8,128,4096]{3,2,1,0:T(8,128)} %get-tuple-element.158, f32[2,8,128]{2,1,0:T(8,128)S(1)} %broadcast_maximum_fusion, pred[128,4096]{1,0:T(8,128)(4,1)S(1)} %fusion.8), kind=kOutput, calls=%fused_computation.3 | convolution fusion | flops 12918456320 | bytes 39329792 | tf_op jit(solution)/shard_map/cond/branch_1_fun/kgqn,nkd->kgqd/dot_general | solution.py:179
  193.2 16.5 %fusion.2 = f32[2,8,128]{2,1,0:T(8,128)S(1)} fusion(f32[2,8,128,4096]{3,2,1,0:T(8,128)} %get-tuple-element.158, f32[2,8,128]{2,1,0:T(8,128)S(1)} %broadcast_maximum_fusion, pred[128,4096]{1,0:T(8,128)(4,1)S(1)} %fusion.8), kind=kLoop, calls=%fused_computation.4 | loop fusion | flops 41940992 | bytes 34095104 | tf_op jit(solution)/shard_map/cond/branch_1_fun/reduce_sum | solution.py:178
  210.4 0.6 copy.101
  211.0 1.3 copy.144
  212.3 142.5 %all-gather.7.cloned.1.call-done = f32[512,128,128]{2,1,0:T(8,128)} async-done(((f32[16,128,128]{2,1,0:T(8,128)}), f32[512,128,128]{2,1,0:T(8,128)}) %all-gather.7.cloned.1.call-update) | async-done | bytes 33554448 | tf_op jit(solution)/shard_map/all_gather | solution.py:15
  354.9 46.4 %while.14 = (s32[]{:T(128)}, f32[16,128,128]{2,1,0:T(8,128)S(1)}, s32[]{:T(128)}, f32[32,16]{1,0:T(8,128)S(1)}, f32[32,16,128,128]{3,2,1,0:T(8,128)}, /*index=5*/s32[]{:T(128)}, s32[]{:T(128)}) while((s32[]{:T(128)}, f32[16,128,128]{2,1,0:T(8,128)S(1)}, s32[]{:T(128)}, f32[32,16]{1,0:T(8,128)S(1)}, f32[32,16,128,128]{3,2,1,0:T(8,128)}, ...), condition=%wide.region_5.6_spmd.clone, body=%wide.region_4.5_spmd.clone.sunk | while | flops 1048580 | bytes 3146025 | solution.py:24
  354.9 1.5 fusion.35
  356.4 1.5 fusion.35
  357.9 1.5 fusion.35
  359.4 1.5 fusion.35
  360.9 1.5 fusion.35
  362.4 1.5 fusion.35
  363.9 1.5 fusion.35
  365.4 1.5 fusion.35
  366.9 1.5 fusion.35
  368.4 1.5 fusion.35
  369.9 1.5 fusion.35
  371.4 1.5 fusion.35
  372.9 1.5 fusion.35
  374.4 1.5 fusion.35
  375.9 1.5 fusion.35
  377.4 1.5 fusion.35
  378.9 1.5 fusion.35
  380.4 1.5 fusion.35
  381.9 1.5 fusion.35
  383.4 1.5 fusion.35
  384.9 1.5 fusion.35
  386.4 1.5 fusion.35
  387.9 1.5 fusion.35
  389.4 1.5 fusion.35
  390.9 1.5 fusion.35
  392.4 1.5 fusion.35
  393.9 1.5 fusion.35
  395.4 1.5 fusion.35
  396.9 1.5 fusion.35
  398.4 1.5 fusion.35
  399.9 1.5 fusion.35
  401.3 1.9 multiply_reduce_fusion
  403.7 2.5 divide_multiply_fusion
  (71 shorter events, 3.9 us)
Async XLA Ops:
  7.2 90.9 %copy-start = (f32[128,2048]{1,0:T(8,128)S(1)}, f32[128,2048]{1,0:T(8,128)}, u32[]{:S(2)}) copy-start(f32[128,2048]{1,0:T(8,128)} %param.14) | copy-start | bytes 3145732
  7.2 111.1 %all-gather.5.cloned.1.call-start = ((), (), s32[]{:S(2)}) async-start(), calls=%async_computation | async-start | bytes 8650752 | tf_op jit(solution)/shard_map/all_gather | solution.py:158
  12.6 342.3 %all-gather.7.cloned.1.call-start = ((), (), s32[]{:S(2)}) async-start(), calls=%async_computation.1 | async-start | bytes 34603008 | tf_op jit(solution)/shard_map/all_gather | solution.py:15
  16.7 4.8 %copy-start.1 = (f32[128,2048]{0,1:T(8,128)}, f32[128,2048]{0,1:T(8,128)S(1)}, u32[]{:S(2)}) copy-start(f32[128,2048]{0,1:T(8,128)S(1)} %copy.111) | copy-start | bytes 3145732
  118.3 285.4 %copy-start.2 = (f32[2048]{0:T(1024)S(1)}, f32[2048]{0:T(1024)}, u32[]{:S(2)}) copy-start(f32[2048]{0:T(1024)} %param.19) | copy-start | bytes 24580
Sparse Core Ops, SparseCore 0:
  12.7 105.4 all-gather.4
  121.4 233.4 all-gather.6
where the time goes:
time: 415 us; the launch traced here: 413 us
  waiting for transfers between devices  158 us (38%)
  matrix products  80.1 us (19%)
  other arithmetic  74 us (18%)
  blocking collectives  65.1 us (16%)
  local copies, waits for them, and re-layouts  18.7 us (5%)
  between operations  15.6 us (4%)
    all_gather x1, waiting for transfers between devices, entering(): pieces = jax.tree.map(lambda part: lax.all_gather(part, axis), value)  143 us
    unnamed x1, blocking collectives  65.1 us
    select_n x31, other arithmetic, turn(): jnp.where(position < mine, new, old)  45.2 us
    dot_general x1, matrix products, attend(): jnp.einsum('kgqd,nkd->kgqn', queries, key_rows, precision=highest) * scale  35.2 us
    dot_general x1, matrix products, attend(): jnp.einsum('kgqn,nkd->kgqd', weights, value_rows, precision=highest)  35.1 us
    reduce_sum x1, other arithmetic, attend(): total_new = jnp.sum(weights, axis=-1)  16.5 us
    all_gather x1, waiting for transfers between devices, shards(): piece = lax.all_gather(stacked, 'context', axis=1, tiled=True)  15.6 us
  transfers between devices with their start and end apart: 2, of which 2 were waited for; matrix products, arithmetic and copies ran while one was open for 28% of the time, Pallas kernels for 0%

commit v1 on v0

--- a/solution.py
+++ b/solution.py
@@ -155,7 +155,9 @@
         jnp.zeros((kv_local, group, rows_here), jnp.float32),
         jnp.zeros((kv_local, group, rows_here, HEAD_DIM), jnp.float32),
     )
-    piece = lax.all_gather(stacked, "context", axis=1, tiled=True)
+    piece = jnp.concatenate(
+        lax.all_to_all(jnp.stack([stacked] * lax.axis_size("context")), "context", 0, 0), axis=1
+    )
     start = jnp.int32(0)
     count = piece.shape[1]
     relevant = (start <= last_token) & (start + count - 1 >= first_begin)

time: 415 us -> 559 us (1.35)
  the two profiles are of different devices: /device:TPU:1 before, /device:TPU:2 now
where the time goes in v1:
time: 559 us; the launch traced here: 549 us
  blocking collectives  320 us (57%)
  matrix products  83.3 us (15%)
  other arithmetic  75.5 us (14%)
  local copies, waits for them, and re-layouts  40.7 us (7%)
  between operations  15.9 us (3%)
  starting transfers between devices  11.7 us (2%)
    unnamed x1, blocking collectives  320 us
    select_n x31, other arithmetic, turn(): jnp.where(position < mine, new, old)  45.2 us
    dot_general x1, matrix products, attend(): jnp.einsum('kgqn,nkd->kgqd', weights, value_rows, precision=highest)  36.4 us
    dot_general x1, matrix products, attend(): jnp.einsum('kgqd,nkd->kgqn', queries, key_rows, precision=highest) * scale  35 us
    reduce_sum x1, other arithmetic, attend(): total_new = jnp.sum(weights, axis=-1)  15.9 us
    all_to_all x1, starting transfers between devices, shards(): lax.all_to_all(jnp.stack([stacked] * lax.axis_size('context')), 'context'...  11.6 us
  transfers between devices with their start and end apart: 2, of which 0 were waited for; matrix products, arithmetic and copies ran while one was open for 25% of the time, Pallas kernels for 0%

profile of v1, /device:TPU:2, one launch (start us, length us, event | category | flops | bytes accessed | tf_op | source)
XLA Modules:
  0.0 548.8 jit_solution(16280913986583332509)
XLA Ops:
  7.2 0.8 copy.58
  8.2 1.4 fusion.25
  10.3 0.6 broadcast_compare_fusion
  11.5 0.7 neg.14
  12.2 1.5 copy.78
  14.0 0.9 slice_reduce_fusion
  15.0 3.4 fusion.18
  18.4 1.0 reshape.350
  20.7 0.9 pad_maximum_fusion.1
  21.7 4.2 stack.8
  25.9 11.6 %all-to-all-start = ((f32[32,2,128,256]{2,3,1,0:T(8,128)}), f32[32,2,128,256]{2,3,1,0:T(8,128)}, u32[]{:S(2)}, u32[]{:S(2)}) async-start(f32[32,2,128,256]{2,3,1,0:T(8,128)} %stack.8), calls=%async_computation | async-start | bytes 16777216 | tf_op jit(solution)/shard_map/all_to_all | solution.py:159
  37.6 1.4 copy.87
  39.3 1.3 copy.83
  41.3 0.7 dynamic-slice
  42.9 320.2 %all-reduce = f32[512]{0:T(512)S(1)} all-reduce(f32[512]{0:T(512)S(1)} %dynamic-update-slice), channel_id=2, replica_groups=mesh['context'=32,'head'=2,'dp'=4] {'context'}, use_global_device_ids=true, to_apply=%add | all-reduce | flops 512 | bytes 4096
  363.2 1.4 copy.86
  365.0 0.6 multiply_subtract_fusion
  365.6 2.9 pad_maximum_fusion
  368.6 2.5 convolution_multiply_fusion
  371.1 3.0 convolution_bitcast_fusion.1
  374.1 111.6 %conditional.1 = (f32[2,8,128]{2,1,0:T(8,128)S(1)}, f32[2,8,128,128]{3,2,1,0:T(8,128)}) conditional(s32[]{:T(128)} %convert_element_type.19, () %tuple.31, (s32[16]{0:T(128)S(1)}, s32[128]{0:T(128)S(1)}, s32[128]{0:T(128)S(1)}, s32[128]{0:T(128)S(1)}, f32[2,32,128,256]{2,3,0,1:T(8,128)}, /*index=5*/f32[2,8,128,128]{3,2,1,0:T(8,128)}) %tuple.67), branch_computations={%region_8.9_spmd, %region_9.13_spmd} | conditional | flops 25872230400 | bytes 163662416 | solution.py:187
  375.1 8.4 %copy.67 = f32[2,32,128,256]{2,1,3,0:T(8,128)S(1)} copy(f32[2,32,128,256]{2,3,0,1:T(8,128)} %get-tuple-element.149) | data formatting | bytes 16777216 | tf_op jit(solution)/shard_map
  383.4 4.4 fusion.26
  387.8 5.5 squeeze.20
  393.3 35.0 %fusion = (f32[2,8,128]{2,1,0:T(8,128)S(1)}, f32[2,8,128,4096]{3,2,1,0:T(8,128)}) fusion(pred[128,4096]{1,0:T(8,128)(4,1)S(1)} %fusion.11, f32[2,8,128,128]{3,2,1,0:T(8,128)} %get-tuple-element.111, f32[4096,2,128]{0,2,1:T(8,128)} %squeeze.20), kind=kOutput, calls=%fused_computation.2 | convolution fusion | flops 12910065664 | bytes 39329792 | tf_op jit(solution)/shard_map/cond/branch_1_fun/kgqd,nkd->kgqn/dot_general | solution.py:176
  428.3 4.9 squeeze.21
  433.2 36.4 %fusion.1 = f32[2,8,128,128]{3,2,1,0:T(8,128)} fusion(f32[2,8,128,4096]{3,2,1,0:T(8,128)} %get-tuple-element.170, f32[2,8,128]{2,1,0:T(8,128)S(1)} %broadcast_maximum_fusion, pred[128,4096]{1,0:T(8,128)(4,1)S(1)} %fusion.11, f32[4096,2,128]{0,2,1:T(8,128)} %squeeze.21), kind=kOutput, calls=%fused_computation.3 | convolution fusion | flops 12918456320 | bytes 39329792 | tf_op jit(solution)/shard_map/cond/branch_1_fun/kgqn,nkd->kgqd/dot_general | solution.py:181
  469.6 15.9 %fusion.2 = f32[2,8,128]{2,1,0:T(8,128)S(1)} fusion(f32[2,8,128,4096]{3,2,1,0:T(8,128)} %get-tuple-element.170, f32[2,8,128]{2,1,0:T(8,128)S(1)} %broadcast_maximum_fusion, pred[128,4096]{1,0:T(8,128)(4,1)S(1)} %fusion.11), kind=kLoop, calls=%fused_computation.4 | loop fusion | flops 41940992 | bytes 34095104 | tf_op jit(solution)/shard_map/cond/branch_1_fun/reduce_sum | solution.py:180
  485.7 1.6 divide_bitcast_fusion
  487.9 1.3 copy.110
  489.2 46.4 %while.14 = (s32[]{:T(128)}, f32[16,128,128]{2,1,0:T(8,128)S(1)}, s32[]{:T(128)}, f32[32,16]{1,0:T(8,128)S(1)}, f32[32,16,128,128]{3,2,1,0:T(8,128)}, /*index=5*/s32[]{:T(128)}, s32[]{:T(128)}) while((s32[]{:T(128)}, f32[16,128,128]{2,1,0:T(8,128)S(1)}, s32[]{:T(128)}, f32[32,16]{1,0:T(8,128)S(1)}, f32[32,16,128,128]{3,2,1,0:T(8,128)}, ...), condition=%wide.region_5.6_spmd.clone, body=%wide.region_4.5_spmd.clone.sunk | while | flops 1048580 | bytes 3146025 | solution.py:24
  489.2 1.5 fusion.36
  490.7 1.5 fusion.36
  492.2 1.5 fusion.36
  493.7 1.5 fusion.36
  495.2 1.5 fusion.36
  496.7 1.5 fusion.36
  498.2 1.5 fusion.36
  499.7 1.5 fusion.36
  501.2 1.5 fusion.36
  502.7 1.5 fusion.36
  504.2 1.5 fusion.36
  505.7 1.5 fusion.36
  507.2 1.5 fusion.36
  508.7 1.5 fusion.36
  510.2 1.5 fusion.36
  511.7 1.5 fusion.36
  513.2 1.5 fusion.36
  514.7 1.5 fusion.36
  516.2 1.5 fusion.36
  517.7 1.5 fusion.36
  519.2 1.5 fusion.36
  520.7 1.5 fusion.36
  522.2 1.5 fusion.36
  523.7 1.5 fusion.36
  525.2 1.5 fusion.36
  526.7 1.5 fusion.36
  528.2 1.5 fusion.36
  529.7 1.5 fusion.36
  531.2 1.5 fusion.36
  532.7 1.5 fusion.36
  534.2 1.5 fusion.36
  535.7 3.1 multiply_reduce_fusion
  539.2 2.5 divide_multiply_fusion
  (76 shorter events, 6.3 us)
Async XLA Ops:
  7.2 361.5 %copy-start = (f32[128,2048]{1,0:T(8,128)S(1)}, f32[128,2048]{1,0:T(8,128)}, u32[]{:S(2)}) copy-start(f32[128,2048]{1,0:T(8,128)} %param.14) | copy-start | bytes 3145732
  7.2 34.2 %copy-start.3 = (u32[256]{0:T(256)S(1)}, u32[256]{0:T(256)}, u32[]{:S(2)}) copy-start(u32[256]{0:T(256)} %constant.80) | copy-start | bytes 3076
  7.2 482.0 %all-gather.4.cloned.1.call-start = ((), (), s32[]{:S(2)}) async-start(), calls=%async_computation.1 | async-start | bytes 34603008 | tf_op jit(solution)/shard_map/all_gather | solution.py:15
  13.7 23.8 %copy-start.1 = (f32[128,2048]{0,1:T(8,128)}, f32[128,2048]{0,1:T(8,128)S(1)}, u32[]{:S(2)}) copy-start(f32[128,2048]{0,1:T(8,128)S(1)} %copy.78) | copy-start | bytes 3145732
  25.9 348.2 %all-to-all-start = ((f32[32,2,128,256]{2,3,1,0:T(8,128)}), f32[32,2,128,256]{2,3,1,0:T(8,128)}, u32[]{:S(2)}, u32[]{:S(2)}) async-start(f32[32,2,128,256]{2,3,1,0:T(8,128)} %stack.8), calls=%async_computation | async-start | bytes 16777216 | tf_op jit(solution)/shard_map/all_to_all | solution.py:159
  374.1 165.1 %copy-start.2 = (f32[2048]{0:T(1024)S(1)}, f32[2048]{0:T(1024)}, u32[]{:S(2)}) copy-start(f32[2048]{0:T(1024)} %param.19) | copy-start | bytes 24580
Sparse Core Ops, SparseCore 0:
  18.5 401.7 all-gather.3
